TPU v7x, 512 devices: a whole 4x4x16 slice. The times are simulated.
512 devices in a mesh: docs: 16 (over y, x), supp: 32 (over z, core).
Axes of the slice: x: 4, y: 4, z: 16, core: 2. Of those that a mesh axis runs over, the one named last changes fastest.
Arguments:
- vocab_table: bfloat16 [100000, 300], P('docs'), may hold values from -0.69140625 to 0.69140625
- support_atoms: bfloat16 [65536, 300], P('supp'), may hold values from -0.69140625 to 0.69140625
- weight_logits: float32 [65536], P('supp'), may hold values from -6 to 6
- word_counts: int32 [32], P('docs'), may hold values from 1 to 600, 11520 in all
- word_shard: int32 [20480, 1], P('docs'), may hold values from 0 to 15; in each aligned block of 1280 rows (0 to 1279, 1280 to 2559, ...) at most 128 rows name the same one
- word_row: int32 [20480], P('docs'), may hold values from 0 to 6249
Outputs:
- row_potential: float32 [32, 640], P('docs')
- col_potential: float32 [32, 65536], P('docs', 'supp')
- new_log_weights: float32 [65536], P('supp')
Inputs may be any that keep to these rules, and one draw needn't show every extreme that they name: `word_shard`: within the 1280 word slots of each index of docs (aligned blocks), no shard number appears more than 128 times, and some number appears exactly 128 times. `word_counts`: the longest document has exactly 600 words.
All inputs are finite; a program needn't handle non-finite values. No bound on the sum of `word_counts` on one device may be relied on, other than what follows from the above.
Results may differ from a plain program's by a relative error of at most 0.0003.
Values may be sent and summed in bfloat16 or wider, within the bound.
No kernel may reach another device: no remote copies, remote signals or barrier semaphores. Data moves between devices by JAX's collectives and lax.ppermute only.
A program may use at most 64 MiB of HBM per device.

v0:
```python
import jax
import jax.numpy as jnp
from jax import lax
from jax.sharding import PartitionSpec as P

ITERS = 2
epsilon = 0.05


def extent_supp(largest, summed):
    global_max = lax.pmax(largest, "supp")
    global_sum = lax.psum(summed * jnp.exp(largest - global_max), "supp")
    return global_max + jnp.log(global_sum)


def fetch_rows(requests, vocab_table):
    return lax.all_to_all(
        vocab_table[lax.all_to_all(requests, "docs", split_axis=0, concat_axis=0, tiled=True)],
        "docs",
        split_axis=0,
        concat_axis=0,
        tiled=True,
    )


def shards(vocab_table, support_atoms, weight_logits, word_counts, word_shard, word_row):
    groups = lax.axis_size("docs")
    supp_count = lax.axis_size("supp")
    docs_here = word_counts.shape[0]
    slot_count = word_row.shape[0]
    doc_slots = slot_count // docs_here
    atom_count = support_atoms.shape[0]
    capacity = supp_count * (
        (5 * slot_count + 4 * groups * supp_count - 1) // (4 * groups * supp_count)
    )
    word_owner = word_shard[:, 0]
    member = (word_owner[:, None] == jnp.arange(groups, dtype=jnp.int32)[None, :]).astype(jnp.int32)
    slot_rank = jnp.sum((jnp.cumsum(member, axis=0) - 1) * member, axis=1)
    requests = jnp.zeros((groups, capacity), jnp.int32).at[word_owner, slot_rank].set(word_row)
    fetched = fetch_rows(requests, vocab_table)
    word_vecs = fetched[word_owner, slot_rank]
    words_sq = jnp.sum(jnp.square(word_vecs.astype(jnp.float32)), axis=1).reshape(
        docs_here, doc_slots
    )
    atoms_sq = jnp.sum(jnp.square(support_atoms.astype(jnp.float32)), axis=1)
    product = jnp.dot(word_vecs, support_atoms.T, preferred_element_type=jnp.float32)
    product = product.reshape(docs_here, doc_slots, atom_count)
    stored = words_sq[:, :, None] + atoms_sq[None, None, :] - 2.0 * product
    logit_max = jnp.max(weight_logits)
    logit_sum = jnp.sum(jnp.exp(weight_logits - logit_max))
    log_base = weight_logits - extent_supp(logit_max, logit_sum)
    live_mask = jnp.arange(doc_slots)[None, :] < word_counts[:, None]
    log_share = -epsilon * jnp.log(word_counts.astype(jnp.float32))

    def column_extent(row_pot, dist_grid):
        scores = (row_pot[:, :, None] - dist_grid) / epsilon
        largest = jnp.max(jnp.where(live_mask[:, :, None], scores, -jnp.inf), axis=1)
        summed = jnp.sum(
            jnp.where(live_mask[:, :, None], jnp.exp(scores - largest[:, None, :]), 0.0), axis=1
        )
        return largest + jnp.log(summed)

    row_pot = jnp.zeros((docs_here, doc_slots), jnp.float32)
    col_pot = jnp.zeros((docs_here, atom_count), jnp.float32)
    for sweep in range(ITERS):
        dist_grid = stored
        col_pot = epsilon * log_base[None, :] - epsilon * column_extent(row_pot, dist_grid)
        scores = (col_pot[:, None, :] - dist_grid) / epsilon
        largest = jnp.max(scores, axis=2)
        summed = jnp.sum(jnp.exp(scores - largest[:, :, None]), axis=2)
        row_ext = extent_supp(largest, summed)
        row_pot = jnp.where(live_mask, log_share[:, None] - epsilon * row_ext, 0.0)
    dist_grid = stored
    log_marg = col_pot / epsilon + column_extent(row_pot, dist_grid)
    grand_total = lax.psum(jnp.sum(log_marg, axis=0), "docs")
    mean_log = grand_total / (docs_here * groups)
    mean_max = jnp.max(mean_log)
    mean_sum = jnp.sum(jnp.exp(mean_log - mean_max))
    new_log = mean_log - extent_supp(mean_max, mean_sum)
    return (row_pot, col_pot, new_log)


def solution(mesh):
    placed = (P("docs", None), P("supp", None), P("supp"), P("docs"), P("docs", None), P("docs"))
    return jax.shard_map(
        shards,
        mesh=mesh,
        in_specs=placed,
        out_specs=(P("docs", None), P("docs", "supp"), P("supp")),
        check_vma=False,
    )
```

profile of v0, /device:TPU:1, one launch (start us, length us, event | category | flops | bytes accessed | tf_op | source)
XLA Modules:
  0.0 547.9 jit_solution(805814266147628978)
XLA Ops:
  0.6 0.7 reduce.6
  1.4 4.5 reduce-window.6
  5.9 0.4 slice_reduce_fusion
  6.3 0.2 reduce-window.9
  6.5 0.1 add_add_fusion
  6.7 0.7 or_reduce_fusion
  7.4 0.7 multiply_reduce_fusion.2
  8.1 0.8 and_reduce_fusion
  8.9 6.0 %scatter_custom_fusion = s32[2048]{0:T(1024)} fusion(s32[1280]{0:T(1024)S(1)} %broadcast_select_fusion, s32[1280]{0:T(1024)} %param.11, s32[]{:T(128)} %constant.16.clone.1), kind=kCustom, calls=%fused_computation.55 | custom fusion | bytes 8704
  14.9 7.6 %all-to-all-start = ((s32[16,1,128]{2,1,0:T(1,128)}), s32[16,1,128]{2,1,0:T(1,128)S(1)}, u32[]{:S(2)}, u32[]{:S(2)}) async-start(s32[16,1,128]{2,1,0:T(1,128)} %bitcast.1), calls=%async_computation | async-start | bytes 16384 | tf_op jit(solution)/shard_map/all_to_all | solution.py:18
  22.5 7.1 %copy.11 = bf16[6250,300]{1,0:T(8,128)(2,1)} copy(bf16[6250,300]{0,1:T(8,128)(2,1)} %param.6) | data formatting | bytes 7500000 | tf_op args[0]
  29.6 0.0 copy-start.3
  29.6 0.0 copy-start.1
  29.6 0.0 copy-start.5
  29.6 0.0 all-to-all-done
  29.6 10.3 %gather_fusion = bf16[2048,300]{1,0:T(8,128)(2,1)S(1)} fusion(bf16[6250,300]{1,0:T(8,128)(2,1)} %copy.11, s32[2048]{0:T(1024)S(1)} %fusion.8), kind=kCustom, calls=%fused_computation | custom fusion | bytes 2465792 | tf_op jit(solution)/shard_map/gather | solution.py:18
  39.9 1.6 copy.12
  41.5 6.7 %all-to-all-start.1 = ((bf16[16,128,300]{1,2,0:T(8,128)(2,1)}), bf16[16,128,300]{1,2,0:T(8,128)(2,1)}, u32[]{:S(2)}, u32[]{:S(2)}) async-start(bf16[16,128,300]{1,2,0:T(8,128)(2,1)} %copy.12), calls=%async_computation.1 | async-start | bytes 2490368 | tf_op jit(solution)/shard_map/all_to_all | solution.py:17
  48.2 0.0 copy-done.3
  48.2 0.6 reduce_max.67
  48.8 54.7 %pmax.28 = f32[]{:T(128)} all-reduce(f32[]{:T(128)} %reduce_max.67), channel_id=1, replica_groups=mesh['docs'=16,'supp'=32] {'supp'}, use_global_device_ids=true, to_apply=%region_1.2 | all-reduce | flops 1 | bytes 8 | tf_op jit(solution)/shard_map/pmax | solution.py:11
  104.9 1.3 exponential_reduce_fusion.3
  106.8 47.9 %psum.35 = f32[]{:T(128)} all-reduce(f32[]{:T(128)S(6)} %mul.57), channel_id=1, replica_groups=mesh['docs'=16,'supp'=32] {'supp'}, use_global_device_ids=true, to_apply=%region_3.4 | all-reduce | flops 1 | bytes 8 | tf_op jit(solution)/shard_map/psum | solution.py:12
  156.0 0.0 copy-done.1
  156.1 0.3 multiply_reduce_fusion
  156.3 0.0 copy-done.5
  156.4 0.1 iota_compare_fusion.2
  156.4 0.0 all-to-all-done.1
  156.4 1.8 copy.13
  158.3 8.1 %gather_fusion.1 = bf16[1280,300]{1,0:T(8,128)(2,1)S(1)} fusion(bf16[16,128,300]{2,1,0:T(8,128)(2,1)S(1)} %copy.13, s32[1280]{0:T(1024)S(1)} %get-tuple-element.3), kind=kCustom, calls=%fused_computation.1 | custom fusion | bytes 1546240 | tf_op jit(solution)/shard_map/gather | solution.py:41
  166.4 6.8 %convolution_multiply_fusion = f32[1280,2048]{1,0:T(8,128)} fusion(bf16[1280,300]{1,0:T(8,128)(2,1)S(1)} %gather_fusion.1, bf16[2048,300]{0,1:T(8,128)(2,1)} %param.7), kind=kOutput, calls=%fused_computation.20 | convolution fusion | flops 1575485440 | bytes 12482560 | tf_op jit(solution)/shard_map/dot_general | solution.py:46
  173.2 0.3 multiply_reduce_fusion.1
  173.5 0.0 copy-start
  173.5 6.1 %select_reduce_fusion.5 = f32[2,2048]{1,0:T(2,128)S(1)} fusion(pred[2,640]{1,0:T(4,128)(4,1)S(1)} %iota_compare_fusion.2, f32[2,640,2048]{2,1,0:T(8,128)} %bitcast.41, f32[2048]{0:T(1024)S(1)} %multiply_reduce_fusion, f32[2,640]{1,0:T(2,128)S(1)} %add.104), kind=kLoop, calls=%fused_computation.17 | loop fusion | flops 15724544 | bytes 10516736 | tf_op jit(solution)/shard_map/reduce_max | solution.py:57
  179.6 0.9 copy-done
  180.5 4.1 select_reduce_fusion.4
  184.7 2.1 fusion.2
  186.7 3.0 exponential_reduce_fusion.1
  189.7 46.8 %pmax.29 = f32[2,640]{1,0:T(2,128)S(1)} all-reduce(f32[2,640]{1,0:T(2,128)S(1)} %reduce_max.70), channel_id=1, replica_groups=mesh['docs'=16,'supp'=32] {'supp'}, use_global_device_ids=true, to_apply=%region_13.14 | all-reduce | flops 1280 | bytes 10240 | tf_op jit(solution)/shard_map/pmax | solution.py:11
  236.5 47.0 %psum.36 = f32[2,640]{1,0:T(2,128)S(1)} all-reduce(f32[2,640]{1,0:T(2,128)S(1)} %exponential_multiply_fusion.1), channel_id=1, replica_groups=mesh['docs'=16,'supp'=32] {'supp'}, use_global_device_ids=true, to_apply=%region_15.16 | all-reduce | flops 1280 | bytes 10240 | tf_op jit(solution)/shard_map/psum | solution.py:12
  283.6 0.1 subtract_select_fusion.1
  283.6 0.0 slice-start
  283.6 6.7 %select_reduce_fusion.3 = f32[2,2048]{1,0:T(2,128)S(1)} fusion(f32[2,640]{1,0:T(2,128)S(1)} %subtract_select_fusion.1, pred[2,640]{1,0:T(4,128)(4,1)S(1)} %iota_compare_fusion.2, f32[2,640,2048]{2,1,0:T(8,128)} %bitcast.42, f32[2048]{0:T(1024)S(1)} %multiply_reduce_fusion, f32[2,640]{1,0:T(2,128)S(1)} %add.104), kind=kLoop, calls=%fused_computation.12 | loop fusion | flops 15724544 | bytes 10521856 | tf_op jit(solution)/shard_map/reduce_max | solution.py:57
  290.3 0.0 slice-start.2
  290.4 6.8 %select_reduce_fusion.2 = f32[2,2048]{1,0:T(2,128)S(1)} fusion(f32[2,2048]{1,0:T(2,128)S(1)} %select_reduce_fusion.3, f32[2,640]{1,0:T(2,128)S(1)} %subtract_select_fusion.1, pred[2,640]{1,0:T(4,128)(4,1)S(1)} %iota_compare_fusion.2, f32[2,640,2048]{2,1,0:T(8,128)} %bitcast.43, f32[2048]{0:T(1024)S(1)} %multiply_reduce_fusion, f32[2,640]{1,0:T(2,128)S(1)} %add.104), kind=kLoop, calls=%fused_computation.11 | loop fusion | flops 18345984 | bytes 10538240 | tf_op jit(solution)/shard_map/reduce_sum | solution.py:58
  297.1 0.0 slice-done
  297.2 0.0 slice-done.1
  297.2 0.0 slice-done.2
  297.2 0.0 copy-start.2
  297.2 2.1 fusion.3
  299.3 3.0 exponential_reduce_fusion
  302.3 46.8 %pmax.30 = f32[2,640]{1,0:T(2,128)S(1)} all-reduce(f32[2,640]{1,0:T(2,128)S(1)} %reduce_max.73), channel_id=1, replica_groups=mesh['docs'=16,'supp'=32] {'supp'}, use_global_device_ids=true, to_apply=%region_19.20 | all-reduce | flops 1280 | bytes 10240 | tf_op jit(solution)/shard_map/pmax | solution.py:11
  349.1 46.8 %psum.37 = f32[2,640]{1,0:T(2,128)S(1)} all-reduce(f32[2,640]{1,0:T(2,128)S(1)} %exponential_multiply_fusion), channel_id=1, replica_groups=mesh['docs'=16,'supp'=32] {'supp'}, use_global_device_ids=true, to_apply=%region_21.22 | all-reduce | flops 1280 | bytes 10240 | tf_op jit(solution)/shard_map/psum | solution.py:12
  395.9 0.1 subtract_select_fusion
  396.0 5.8 %select_reduce_fusion.1 = f32[2,2048]{1,0:T(2,128)S(1)} fusion(f32[2,640]{1,0:T(2,128)S(1)} %subtract_select_fusion, pred[2,640]{1,0:T(4,128)(4,1)S(1)} %iota_compare_fusion.2, f32[2,640,2048]{2,1,0:T(8,128)} %bitcast.44, f32[2048]{0:T(1024)S(1)} %multiply_reduce_fusion, f32[2,640]{1,0:T(2,128)S(1)} %add.104), kind=kLoop, calls=%fused_computation.8 | loop fusion | flops 15724544 | bytes 10521856 | tf_op jit(solution)/shard_map/reduce_max | solution.py:57
  401.7 6.6 %select_reduce_fusion = f32[2,2048]{1,0:T(2,128)S(1)} fusion(f32[2,2048]{1,0:T(2,128)S(1)} %select_reduce_fusion.1, f32[2,640]{1,0:T(2,128)S(1)} %subtract_select_fusion, pred[2,640]{1,0:T(4,128)(4,1)S(1)} %iota_compare_fusion.2, f32[2,640,2048]{2,1,0:T(8,128)} %bitcast.45, f32[2048]{0:T(1024)S(1)} %multiply_reduce_fusion, f32[2,640]{1,0:T(2,128)S(1)} %add.104), kind=kLoop, calls=%fused_computation.7 | loop fusion | flops 18345984 | bytes 10538240 | tf_op jit(solution)/shard_map/reduce_sum | solution.py:58
  408.4 0.0 copy-done.2
  408.4 0.0 copy-done.4
  408.4 33.7 %psum.38 = f32[2048]{0:T(1024)S(1)} all-reduce(f32[2048]{0:T(1024)S(1)} %add_reduce_fusion), channel_id=1, replica_groups=mesh['docs'=16,'supp'=32] {'docs'}, use_global_device_ids=true, to_apply=%region_25.26 | all-reduce | flops 2048 | bytes 16384 | tf_op jit(solution)/shard_map/psum | solution.py:75
  442.1 0.6 multiply_reduce_fusion.3
  442.7 53.8 %pmax.31 = f32[]{:T(128)} all-reduce(f32[]{:T(128)} %multiply_reduce_fusion.3), channel_id=1, replica_groups=mesh['docs'=16,'supp'=32] {'supp'}, use_global_device_ids=true, to_apply=%region_27.28 | all-reduce | flops 1 | bytes 8 | tf_op jit(solution)/shard_map/pmax | solution.py:11
  496.4 1.2 exponential_reduce_fusion.2
  499.6 46.3 %psum.39 = f32[]{:T(128)} all-reduce(f32[]{:T(128)S(6)} %mul.69), channel_id=1, replica_groups=mesh['docs'=16,'supp'=32] {'supp'}, use_global_device_ids=true, to_apply=%region_29.30 | all-reduce | flops 1 | bytes 8 | tf_op jit(solution)/shard_map/psum | solution.py:12
  547.3 0.6 multiply_subtract_fusion.2
  (19 shorter events, 0.2 us)
Async XLA Ops:
  14.9 14.7 %all-to-all-start = ((s32[16,1,128]{2,1,0:T(1,128)}), s32[16,1,128]{2,1,0:T(1,128)S(1)}, u32[]{:S(2)}, u32[]{:S(2)}) async-start(s32[16,1,128]{2,1,0:T(1,128)} %bitcast.1), calls=%async_computation | async-start | bytes 16384 | tf_op jit(solution)/shard_map/all_to_all | solution.py:18
  29.6 18.6 %copy-start.3 = (f32[2048]{0:T(1024)S(1)}, f32[2048]{0:T(1024)}, u32[]{:S(2)}) copy-start(f32[2048]{0:T(1024)} %param.8) | copy-start | bytes 24580
  29.6 126.4 %copy-start.1 = (bf16[2048,300]{0,1:T(8,128)(2,1)S(1)}, bf16[2048,300]{0,1:T(8,128)(2,1)}, u32[]{:S(2)}) copy-start(bf16[2048,300]{0,1:T(8,128)(2,1)} %param.7) | copy-start | bytes 3686404
  29.6 126.7 %copy-start.5 = (s32[2]{0:T(128)S(1)}, s32[2]{0:T(128)}, u32[]{:S(2)}) copy-start(s32[2]{0:T(128)} %param.9) | copy-start | bytes 28
  41.5 114.9 %all-to-all-start.1 = ((bf16[16,128,300]{1,2,0:T(8,128)(2,1)}), bf16[16,128,300]{1,2,0:T(8,128)(2,1)}, u32[]{:S(2)}, u32[]{:S(2)}) async-start(bf16[16,128,300]{1,2,0:T(8,128)(2,1)} %copy.12), calls=%async_computation.1 | async-start | bytes 2490368 | tf_op jit(solution)/shard_map/all_to_all | solution.py:17
  173.5 7.0 %copy-start = (f32[1280,2048]{1,0:T(8,128)S(1)}, f32[1280,2048]{1,0:T(8,128)}, u32[]{:S(2)}) copy-start(f32[1280,2048]{1,0:T(8,128)} %convolution_multiply_fusion) | copy-start | bytes 31457284
  283.6 13.5 %slice-start = ((s8[10485760]{0:T(1024)(128)(4,1)}), s8[4194304]{0:T(1024)(128)(4,1)S(1)}, s32[]{:S(2)}) async-start(s8[10485760]{0:T(1024)(128)(4,1)} %bitcast.47), calls=%async_computation.2 | async-start | bytes 8388608
  283.6 13.5 %slice-start.1 = ((s8[10485760]{0:T(1024)(128)(4,1)}), s8[4194304]{0:T(1024)(128)(4,1)S(1)}, s32[]{:S(2)}) async-start(s8[10485760]{0:T(1024)(128)(4,1)} %bitcast.47), calls=%async_computation.3 | async-start | bytes 8388608
  290.3 6.8 %slice-start.2 = ((s8[10485760]{0:T(1024)(128)(4,1)}), s8[2097152]{0:T(1024)(128)(4,1)S(1)}, s32[]{:S(2)}) async-start(s8[10485760]{0:T(1024)(128)(4,1)} %bitcast.47), calls=%async_computation.4 | async-start | bytes 4194304
  297.2 111.2 %copy-start.2 = (f32[2,2048]{1,0:T(2,128)}, f32[2,2048]{1,0:T(2,128)S(1)}, u32[]{:S(2)}) copy-start(f32[2,2048]{1,0:T(2,128)S(1)} %multiply_subtract_fusion) | copy-start | bytes 49156
  396.0 12.4 %copy-start.4 = (f32[2,640]{1,0:T(2,128)}, f32[2,640]{1,0:T(2,128)S(1)}, u32[]{:S(2)}) copy-start(f32[2,640]{1,0:T(2,128)S(1)} %subtract_select_fusion) | copy-start | bytes 15364
where the time goes:
time: 549 us; the launch traced here: 548 us
  blocking collectives  424 us (77%)
  other arithmetic  59.1 us (11%)
  local copies, waits for them, and re-layouts  36.3 us (7%)
  starting transfers between devices  14.3 us (3%)
  between operations  7.63 us (1%)
  matrix products  6.83 us (1%)
    pmax x4, blocking collectives, extent_supp(): global_max = lax.pmax(largest, 'supp')  202 us
    psum x4, blocking collectives, extent_supp(): global_sum = lax.psum(summed * jnp.exp(largest - global_max), 'supp')  188 us
    psum x1, blocking collectives, shards(): grand_total = lax.psum(jnp.sum(log_marg, axis=0), 'docs')  33.7 us
    reduce_max x3, other arithmetic, column_extent(): jnp.max(jnp.where(live_mask[:, :, None], scores, -jnp.inf), axis=1)  18.5 us
    reduce_sum x3, other arithmetic, column_extent(): jnp.sum(jnp.where(live_mask[:, :, None], jnp.exp(scores - largest[:, None...  17.5 us
    unnamed x20, local copies, waits for them, and re-layouts  14.1 us
    gather x2, local copies, waits for them, and re-layouts, fetch_rows(): vocab_table[lax.all_to_all(requests, 'docs', split_axis=0, concat_axis=0,...  11.9 us
  transfers between devices with their start and end apart: 2, of which 0 were waited for; matrix products, arithmetic and copies ran while one was open for 2% of the time, Pallas kernels for 0%

commit v1 on v0

--- a/solution.py
+++ b/solution.py
@@ -72,7 +72,7 @@
         row_pot = jnp.where(live_mask, log_share[:, None] - epsilon * row_ext, 0.0)
     dist_grid = stored
     log_marg = col_pot / epsilon + column_extent(row_pot, dist_grid)
-    grand_total = lax.psum(jnp.sum(log_marg, axis=0), "docs")
+    grand_total = jnp.sum(lax.all_gather(jnp.sum(log_marg, axis=0), "docs"), axis=0)
     mean_log = grand_total / (docs_here * groups)
     mean_max = jnp.max(mean_log)
     mean_sum = jnp.sum(jnp.exp(mean_log - mean_max))

time: 549 us -> 532 us (0.969)
  blocking collectives: 424 us -> 407 us
    psum x1 -> x0, blocking collectives: 33.7 us -> none  [shards(): grand_total = lax.psum(jnp.sum(log_marg, axis=0), 'docs')]
    all_gather x0 -> x1, blocking collectives: none -> 18.6 us  [shards(): lax.all_gather(jnp.sum(log_marg, axis=0), 'docs')]
where the time goes in v1:
time: 532 us; the launch traced here: 531 us
  blocking collectives  407 us (77%)
  other arithmetic  59.1 us (11%)
  local copies, waits for them, and re-layouts  36.4 us (7%)
  starting transfers between devices  14.3 us (3%)
  between operations  7.63 us (1%)
  matrix products  6.83 us (1%)
    pmax x4, blocking collectives, extent_supp(): global_max = lax.pmax(largest, 'supp')  200 us
    psum x4, blocking collectives, extent_supp(): global_sum = lax.psum(summed * jnp.exp(largest - global_max), 'supp')  188 us
    all_gather x1, blocking collectives, shards(): lax.all_gather(jnp.sum(log_marg, axis=0), 'docs')  18.6 us
    reduce_max x3, other arithmetic, column_extent(): jnp.max(jnp.where(live_mask[:, :, None], scores, -jnp.inf), axis=1)  18.5 us
    reduce_sum x3, other arithmetic, column_extent(): jnp.sum(jnp.where(live_mask[:, :, None], jnp.exp(scores - largest[:, None...  17.5 us
    unnamed x20, local copies, waits for them, and re-layouts  14.1 us
    gather x2, local copies, waits for them, and re-layouts, fetch_rows(): vocab_table[lax.all_to_all(requests, 'docs', split_axis=0, concat_axis=0,...  11.9 us
  transfers between devices with their start and end apart: 2, of which 0 were waited for; matrix products, arithmetic and copies ran while one was open for 2% of the time, Pallas kernels for 0%

profile of v1, /device:TPU:1, one launch (start us, length us, event | category | flops | bytes accessed | tf_op | source)
XLA Modules:
  0.0 530.8 jit_solution(18399695450374558582)
XLA Ops:
  0.6 0.7 reduce.6
  1.4 4.5 reduce-window.6
  5.9 0.4 slice_reduce_fusion
  6.3 0.2 reduce-window.9
  6.5 0.1 add_add_fusion
  6.7 0.7 or_reduce_fusion
  7.4 0.7 multiply_reduce_fusion.2
  8.1 0.8 and_reduce_fusion
  8.9 6.0 %scatter_custom_fusion = s32[2048]{0:T(1024)} fusion(s32[1280]{0:T(1024)S(1)} %broadcast_select_fusion, s32[1280]{0:T(1024)} %param.11, s32[]{:T(128)} %constant.16.clone.1), kind=kCustom, calls=%fused_computation.55 | custom fusion | bytes 8704
  14.9 7.6 %all-to-all-start = ((s32[16,1,128]{2,1,0:T(1,128)}), s32[16,1,128]{2,1,0:T(1,128)S(1)}, u32[]{:S(2)}, u32[]{:S(2)}) async-start(s32[16,1,128]{2,1,0:T(1,128)} %bitcast.1), calls=%async_computation | async-start | bytes 16384 | tf_op jit(solution)/shard_map/all_to_all | solution.py:18
  22.5 7.1 %copy.14 = bf16[6250,300]{1,0:T(8,128)(2,1)} copy(bf16[6250,300]{0,1:T(8,128)(2,1)} %param.6) | data formatting | bytes 7500000 | tf_op args[0]
  29.6 0.0 copy-start.3
  29.6 0.0 copy-start.1
  29.6 0.0 copy-start.5
  29.6 0.0 all-to-all-done
  29.6 10.3 %gather_fusion = bf16[2048,300]{1,0:T(8,128)(2,1)S(1)} fusion(bf16[6250,300]{1,0:T(8,128)(2,1)} %copy.14, s32[2048]{0:T(1024)S(1)} %fusion.8), kind=kCustom, calls=%fused_computation | custom fusion | bytes 2465792 | tf_op jit(solution)/shard_map/gather | solution.py:18
  39.9 1.6 copy.15
  41.5 6.7 %all-to-all-start.1 = ((bf16[16,128,300]{1,2,0:T(8,128)(2,1)}), bf16[16,128,300]{1,2,0:T(8,128)(2,1)}, u32[]{:S(2)}, u32[]{:S(2)}) async-start(bf16[16,128,300]{1,2,0:T(8,128)(2,1)} %copy.15), calls=%async_computation.1 | async-start | bytes 2490368 | tf_op jit(solution)/shard_map/all_to_all | solution.py:17
  48.2 0.0 copy-done.3
  48.2 0.6 reduce_max.67
  48.8 54.7 %pmax.28 = f32[]{:T(128)} all-reduce(f32[]{:T(128)} %reduce_max.67), channel_id=1, replica_groups=mesh['docs'=16,'supp'=32] {'supp'}, use_global_device_ids=true, to_apply=%region_1.2 | all-reduce | flops 1 | bytes 8 | tf_op jit(solution)/shard_map/pmax | solution.py:11
  104.9 1.3 exponential_reduce_fusion.3
  106.8 47.9 %psum.28 = f32[]{:T(128)} all-reduce(f32[]{:T(128)S(6)} %mul.57), channel_id=1, replica_groups=mesh['docs'=16,'supp'=32] {'supp'}, use_global_device_ids=true, to_apply=%region_3.4 | all-reduce | flops 1 | bytes 8 | tf_op jit(solution)/shard_map/psum | solution.py:12
  156.0 0.0 copy-done.1
  156.1 0.3 multiply_reduce_fusion
  156.3 0.0 copy-done.5
  156.4 0.1 iota_compare_fusion.2
  156.4 0.0 all-to-all-done.1
  156.4 1.8 copy.16
  158.3 8.1 %gather_fusion.1 = bf16[1280,300]{1,0:T(8,128)(2,1)S(1)} fusion(bf16[16,128,300]{2,1,0:T(8,128)(2,1)S(1)} %copy.16, s32[1280]{0:T(1024)S(1)} %get-tuple-element.3), kind=kCustom, calls=%fused_computation.1 | custom fusion | bytes 1546240 | tf_op jit(solution)/shard_map/gather | solution.py:41
  166.4 6.8 %convolution_multiply_fusion = f32[1280,2048]{1,0:T(8,128)} fusion(bf16[1280,300]{1,0:T(8,128)(2,1)S(1)} %gather_fusion.1, bf16[2048,300]{0,1:T(8,128)(2,1)} %param.7), kind=kOutput, calls=%fused_computation.20 | convolution fusion | flops 1575485440 | bytes 12482560 | tf_op jit(solution)/shard_map/dot_general | solution.py:46
  173.2 0.3 multiply_reduce_fusion.1
  173.5 0.0 copy-start
  173.5 6.1 %select_reduce_fusion.5 = f32[2,2048]{1,0:T(2,128)S(1)} fusion(pred[2,640]{1,0:T(4,128)(4,1)S(1)} %iota_compare_fusion.2, f32[2,640,2048]{2,1,0:T(8,128)} %bitcast.41, f32[2048]{0:T(1024)S(1)} %multiply_reduce_fusion, f32[2,640]{1,0:T(2,128)S(1)} %add.102), kind=kLoop, calls=%fused_computation.17 | loop fusion | flops 15724544 | bytes 10516736 | tf_op jit(solution)/shard_map/reduce_max | solution.py:57
  179.6 0.9 copy-done
  180.5 4.1 select_reduce_fusion.4
  184.7 2.1 fusion.2
  186.7 3.0 exponential_reduce_fusion.1
  189.7 46.8 %pmax.29 = f32[2,640]{1,0:T(2,128)S(1)} all-reduce(f32[2,640]{1,0:T(2,128)S(1)} %reduce_max.70), channel_id=1, replica_groups=mesh['docs'=16,'supp'=32] {'supp'}, use_global_device_ids=true, to_apply=%region_13.14 | all-reduce | flops 1280 | bytes 10240 | tf_op jit(solution)/shard_map/pmax | solution.py:11
  236.5 47.0 %psum.29 = f32[2,640]{1,0:T(2,128)S(1)} all-reduce(f32[2,640]{1,0:T(2,128)S(1)} %exponential_multiply_fusion.1), channel_id=1, replica_groups=mesh['docs'=16,'supp'=32] {'supp'}, use_global_device_ids=true, to_apply=%region_15.16 | all-reduce | flops 1280 | bytes 10240 | tf_op jit(solution)/shard_map/psum | solution.py:12
  283.5 0.1 subtract_select_fusion.1
  283.6 0.0 slice-start
  283.6 6.7 %select_reduce_fusion.3 = f32[2,2048]{1,0:T(2,128)S(1)} fusion(f32[2,640]{1,0:T(2,128)S(1)} %subtract_select_fusion.1, pred[2,640]{1,0:T(4,128)(4,1)S(1)} %iota_compare_fusion.2, f32[2,640,2048]{2,1,0:T(8,128)} %bitcast.42, f32[2048]{0:T(1024)S(1)} %multiply_reduce_fusion, f32[2,640]{1,0:T(2,128)S(1)} %add.102), kind=kLoop, calls=%fused_computation.12 | loop fusion | flops 15724544 | bytes 10521856 | tf_op jit(solution)/shard_map/reduce_max | solution.py:57
  290.3 0.0 slice-start.2
  290.3 6.7 %select_reduce_fusion.2 = f32[2,2048]{1,0:T(2,128)S(1)} fusion(f32[2,2048]{1,0:T(2,128)S(1)} %select_reduce_fusion.3, f32[2,640]{1,0:T(2,128)S(1)} %subtract_select_fusion.1, pred[2,640]{1,0:T(4,128)(4,1)S(1)} %iota_compare_fusion.2, f32[2,640,2048]{2,1,0:T(8,128)} %bitcast.43, f32[2048]{0:T(1024)S(1)} %multiply_reduce_fusion, f32[2,640]{1,0:T(2,128)S(1)} %add.102), kind=kLoop, calls=%fused_computation.11 | loop fusion | flops 18345984 | bytes 10538240 | tf_op jit(solution)/shard_map/reduce_sum | solution.py:58
  297.1 0.0 slice-done
  297.1 0.0 slice-done.1
  297.1 0.0 slice-done.2
  297.2 0.0 copy-start.2
  297.2 2.1 fusion.3
  299.2 3.0 exponential_reduce_fusion
  302.2 46.8 %pmax.30 = f32[2,640]{1,0:T(2,128)S(1)} all-reduce(f32[2,640]{1,0:T(2,128)S(1)} %reduce_max.73), channel_id=1, replica_groups=mesh['docs'=16,'supp'=32] {'supp'}, use_global_device_ids=true, to_apply=%region_19.20 | all-reduce | flops 1280 | bytes 10240 | tf_op jit(solution)/shard_map/pmax | solution.py:11
  349.1 46.8 %psum.30 = f32[2,640]{1,0:T(2,128)S(1)} all-reduce(f32[2,640]{1,0:T(2,128)S(1)} %exponential_multiply_fusion), channel_id=1, replica_groups=mesh['docs'=16,'supp'=32] {'supp'}, use_global_device_ids=true, to_apply=%region_21.22 | all-reduce | flops 1280 | bytes 10240 | tf_op jit(solution)/shard_map/psum | solution.py:12
  395.9 0.1 subtract_select_fusion
  395.9 5.8 %select_reduce_fusion.1 = f32[2,2048]{1,0:T(2,128)S(1)} fusion(f32[2,640]{1,0:T(2,128)S(1)} %subtract_select_fusion, pred[2,640]{1,0:T(4,128)(4,1)S(1)} %iota_compare_fusion.2, f32[2,640,2048]{2,1,0:T(8,128)} %bitcast.44, f32[2048]{0:T(1024)S(1)} %multiply_reduce_fusion, f32[2,640]{1,0:T(2,128)S(1)} %add.102), kind=kLoop, calls=%fused_computation.8 | loop fusion | flops 15724544 | bytes 10521856 | tf_op jit(solution)/shard_map/reduce_max | solution.py:57
  401.7 6.6 %select_reduce_fusion = f32[2,2048]{1,0:T(2,128)S(1)} fusion(f32[2,2048]{1,0:T(2,128)S(1)} %select_reduce_fusion.1, f32[2,640]{1,0:T(2,128)S(1)} %subtract_select_fusion, pred[2,640]{1,0:T(4,128)(4,1)S(1)} %iota_compare_fusion.2, f32[2,640,2048]{2,1,0:T(8,128)} %bitcast.45, f32[2048]{0:T(1024)S(1)} %multiply_reduce_fusion, f32[2,640]{1,0:T(2,128)S(1)} %add.102), kind=kLoop, calls=%fused_computation.7 | loop fusion | flops 18345984 | bytes 10538240 | tf_op jit(solution)/shard_map/reduce_sum | solution.py:58
  408.3 0.0 copy-done.2
  408.3 0.0 copy-done.4
  408.4 18.6 %all-gather = f32[32768]{0:T(1024)S(1)} all-gather(f32[2048]{0:T(1024)S(1)} %add_reduce_fusion), channel_id=2, replica_groups=mesh['docs'=16,'supp'=32] {'docs'}, dimensions={0}, use_global_device_ids=true | all-gather | bytes 139264 | tf_op jit(solution)/shard_map/all_gather | solution.py:75
  427.0 0.6 multiply_reduce_fusion.3
  427.6 51.7 %pmax.31 = f32[]{:T(128)} all-reduce(f32[]{:T(128)} %multiply_reduce_fusion.3), channel_id=1, replica_groups=mesh['docs'=16,'supp'=32] {'supp'}, use_global_device_ids=true, to_apply=%region_27.28 | all-reduce | flops 1 | bytes 8 | tf_op jit(solution)/shard_map/pmax | solution.py:11
  479.4 1.2 exponential_reduce_fusion.2
  482.5 46.3 %psum.31 = f32[]{:T(128)} all-reduce(f32[]{:T(128)S(6)} %mul.69), channel_id=1, replica_groups=mesh['docs'=16,'supp'=32] {'supp'}, use_global_device_ids=true, to_apply=%region_29.30 | all-reduce | flops 1 | bytes 8 | tf_op jit(solution)/shard_map/psum | solution.py:12
  530.2 0.6 multiply_subtract_fusion.2
  (21 shorter events, 0.3 us)
Async XLA Ops:
  14.9 14.7 %all-to-all-start = ((s32[16,1,128]{2,1,0:T(1,128)}), s32[16,1,128]{2,1,0:T(1,128)S(1)}, u32[]{:S(2)}, u32[]{:S(2)}) async-start(s32[16,1,128]{2,1,0:T(1,128)} %bitcast.1), calls=%async_computation | async-start | bytes 16384 | tf_op jit(solution)/shard_map/all_to_all | solution.py:18
  29.6 18.6 %copy-start.3 = (f32[2048]{0:T(1024)S(1)}, f32[2048]{0:T(1024)}, u32[]{:S(2)}) copy-start(f32[2048]{0:T(1024)} %param.8) | copy-start | bytes 24580
  29.6 126.4 %copy-start.1 = (bf16[2048,300]{0,1:T(8,128)(2,1)S(1)}, bf16[2048,300]{0,1:T(8,128)(2,1)}, u32[]{:S(2)}) copy-start(bf16[2048,300]{0,1:T(8,128)(2,1)} %param.7) | copy-start | bytes 3686404
  29.6 126.7 %copy-start.5 = (s32[2]{0:T(128)S(1)}, s32[2]{0:T(128)}, u32[]{:S(2)}) copy-start(s32[2]{0:T(128)} %param.9) | copy-start | bytes 28
  41.5 114.9 %all-to-all-start.1 = ((bf16[16,128,300]{1,2,0:T(8,128)(2,1)}), bf16[16,128,300]{1,2,0:T(8,128)(2,1)}, u32[]{:S(2)}, u32[]{:S(2)}) async-start(bf16[16,128,300]{1,2,0:T(8,128)(2,1)} %copy.15), calls=%async_computation.1 | async-start | bytes 2490368 | tf_op jit(solution)/shard_map/all_to_all | solution.py:17
  173.5 7.0 %copy-start = (f32[1280,2048]{1,0:T(8,128)S(1)}, f32[1280,2048]{1,0:T(8,128)}, u32[]{:S(2)}) copy-start(f32[1280,2048]{1,0:T(8,128)} %convolution_multiply_fusion) | copy-start | bytes 31457284
  283.6 13.5 %slice-start = ((s8[10485760]{0:T(1024)(128)(4,1)}), s8[4194304]{0:T(1024)(128)(4,1)S(1)}, s32[]{:S(2)}) async-start(s8[10485760]{0:T(1024)(128)(4,1)} %bitcast.47), calls=%async_computation.2 | async-start | bytes 8388608
  283.6 13.5 %slice-start.1 = ((s8[10485760]{0:T(1024)(128)(4,1)}), s8[4194304]{0:T(1024)(128)(4,1)S(1)}, s32[]{:S(2)}) async-start(s8[10485760]{0:T(1024)(128)(4,1)} %bitcast.47), calls=%async_computation.3 | async-start | bytes 8388608
  290.3 6.8 %slice-start.2 = ((s8[10485760]{0:T(1024)(128)(4,1)}), s8[2097152]{0:T(1024)(128)(4,1)S(1)}, s32[]{:S(2)}) async-start(s8[10485760]{0:T(1024)(128)(4,1)} %bitcast.47), calls=%async_computation.4 | async-start | bytes 4194304
  297.2 111.2 %copy-start.2 = (f32[2,2048]{1,0:T(2,128)}, f32[2,2048]{1,0:T(2,128)S(1)}, u32[]{:S(2)}) copy-start(f32[2,2048]{1,0:T(2,128)S(1)} %multiply_subtract_fusion) | copy-start | bytes 49156
  395.9 12.4 %copy-start.4 = (f32[2,640]{1,0:T(2,128)}, f32[2,640]{1,0:T(2,128)S(1)}, u32[]{:S(2)}) copy-start(f32[2,640]{1,0:T(2,128)S(1)} %subtract_select_fusion) | copy-start | bytes 15364
